TPU v7x, 32 devices: a whole 2x2x4 slice. The times are simulated.
32 devices in a mesh: col: 8 (over y, x, core), row: 4 (over z).
Axes of the slice: x: 2, y: 2, z: 4, core: 2. Of those that a mesh axis runs over, the one named last changes fastest.
Arguments:
- samples_x: bfloat16 [512, 98304], P('row', 'col'), may hold values from -6 to 6
- targets: bfloat16 [512, 98304], P('row', 'col'), may hold values from -6 to 6
- times: int32 [512], P('row'), may hold values from 0 to 63
- block_rows: int32 [576], P(('col', 'row')), may hold values from 0 to 767, as said below
- block_cols: int32 [576], P(('col', 'row')), may hold values from 0 to 767, as said below
Outputs:
- coeffs: float32 [576, 128, 128], P(('col', 'row'))
- residual: float32 [512, 98304], P('row', 'col')
Inputs may be any that keep to these rules, and one draw needn't show every extreme that they name: `block_rows`: the blocks are listed by column group (the 96 column blocks c * 96 to (c + 1) * 96 - 1 form group c), and within a group in 8 runs of 9 blocks, run g holding row blocks of group g; no block appears twice. `block_cols`: each block's column block lies in the group of its place in the list, as described for block_rows.
All inputs are finite; a program needn't handle non-finite values.
Results may differ from a plain program's by a relative error of at most 0.009.
Values may be sent and summed in bfloat16 or wider, within the bound.
A program may use at most 192 MiB of HBM per device.

v0:
```python
import jax
import jax.numpy as jnp
from jax import lax
from jax.sharding import PartitionSpec as P

BLOCK = 128
ITERS = 2
T_STEPS = 64


RIDGE_SHARE = 0.2


def take_blocks(source, rows_local):
    samples = source.shape[0]
    shaped = source.reshape(samples, source.shape[1] // BLOCK, BLOCK)
    return jnp.take(shaped, rows_local, axis=1)


def block_products(x_blocks, e_blocks):
    return jnp.einsum("ska,skb->kab", x_blocks, e_blocks, preferred_element_type=jnp.float32)


def column_sums(x_blocks, directions, cols_local, column_count):
    contrib = jnp.einsum("ska,kab->skb", x_blocks, directions, preferred_element_type=jnp.float32)
    onehot = (cols_local[:, None] == jnp.arange(column_count, dtype=jnp.int32)[None, :]).astype(
        jnp.float32
    )
    summed = jnp.einsum("skb,kc->scb", contrib, onehot, precision=lax.Precision.HIGHEST)
    return summed.reshape(summed.shape[0], column_count * BLOCK)


def on_device(samples_x, targets, times, block_rows, block_cols):
    col_count = lax.axis_size("col")
    row_count = lax.axis_size("row")
    taxa_col = samples_x.shape[1]
    sample_count = samples_x.shape[0]
    column_count = taxa_col // BLOCK
    my_col = lax.axis_index("col")
    weight = (0.5 + times.astype(jnp.float32) / T_STEPS)[:, None]
    ridge = RIDGE_SHARE * sample_count * row_count
    shard_blocks = block_rows.shape[0]
    group_count = shard_blocks * row_count
    run_length = group_count // col_count
    rows_group, cols_group = (
        lax.all_gather(block_rows, "row", axis=0, tiled=True),
        lax.all_gather(block_cols, "row", axis=0, tiled=True),
    )
    cols_local = cols_group - my_col * column_count
    empty_terms = jnp.zeros((group_count, BLOCK, BLOCK), jnp.float32)
    start_weighted = (targets.astype(jnp.float32) * weight).astype(jnp.bfloat16)
    first_e = take_blocks(start_weighted, cols_local)
    piece = lax.all_gather(samples_x, "col", axis=1, tiled=True)
    terms = empty_terms
    adjoint_terms = terms
    start = jnp.int32(0)
    found = []
    for k in range(piece.shape[1] // taxa_col):
        group = start // taxa_col + k
        runs_first = group * run_length
        shard = piece[:, k * taxa_col : (k + 1) * taxa_col]
        rows_run = (
            lax.dynamic_slice_in_dim(rows_group, runs_first, run_length) - group * column_count
        )
        found.append((runs_first, take_blocks(shard, rows_run)))
    for first, x_run in found:
        e_run = lax.dynamic_slice_in_dim(first_e, first, run_length, 1)
        adjoint_terms = lax.dynamic_update_slice_in_dim(
            adjoint_terms, block_products(x_run, e_run), first, 0
        )
    terms = adjoint_terms
    sample_terms = terms
    stash_blocks = take_blocks(piece, rows_group)

    def reduce_terms(terms):
        return lax.psum_scatter(
            terms.astype(jnp.bfloat16), "row", scatter_dimension=0, tiled=True
        ).astype(jnp.float32)

    share = 1.0

    def norm_of(gradient):
        return lax.psum(share * jnp.sum(gradient * gradient), ("col", "row"))

    gradient = reduce_terms(sample_terms)
    gamma = norm_of(gradient)
    direction = gradient.astype(jnp.bfloat16)
    coeffs = jnp.zeros(gradient.shape, jnp.float32)
    residual = targets.astype(jnp.float32)
    for step in range(ITERS):
        image = column_sums(
            stash_blocks,
            lax.all_gather(direction, "row", axis=0, tiled=True),
            cols_local,
            column_count,
        )
        flat = direction.astype(jnp.float32)
        image_norm, direction_norm = lax.psum(
            (jnp.sum(weight * image * image), share * jnp.sum(flat * flat)), ("col", "row")
        )
        alpha = gamma / (image_norm + ridge * direction_norm)
        coeffs = coeffs + alpha * flat
        residual = residual - alpha * image
        if step + 1 < ITERS:
            e_blocks = take_blocks((residual * weight).astype(jnp.bfloat16), cols_local)
            gradient = reduce_terms(block_products(stash_blocks, e_blocks)) - ridge * coeffs
            gamma_next = norm_of(gradient)
            direction = (gradient + gamma_next / gamma * flat).astype(jnp.bfloat16)
            gamma = gamma_next
    return (coeffs, residual)


def solution(mesh):
    placed = (P("row", "col"), P("row", "col"), P("row"), P(("col", "row")), P(("col", "row")))
    return jax.shard_map(
        on_device,
        mesh=mesh,
        in_specs=placed,
        out_specs=(P(("col", "row"), None, None), P("row", "col")),
        check_vma=False,
    )
```

profile of v0, /device:TPU:0, one launch (start us, length us, event | category | flops | bytes accessed | tf_op | source)
XLA Modules:
  0.0 667.3 jit_solution(10103814361667231141)
XLA Ops:
  7.2 4.7 copy.45
  12.0 3.5 copy.47
  15.5 2.0 fusion
  17.5 4.7 copy.48
  22.2 0.6 dynamic-slice
  23.9 10.1 %all-reduce.3 = (s32[72]{0:T(128)S(1)}, s32[72]{0:T(128)S(1)}) all-reduce(s32[72]{0:T(128)S(1)} %dynamic-update-slice.1, s32[72]{0:T(128)S(1)} %dynamic-update-slice), channel_id=1, replica_groups=mesh['col'=8,'row'=4] {'row'}, use_global_device_ids=true, to_apply=%add.2 | all-reduce | flops 144 | bytes 1152
  34.0 4.3 gather_fusion.2
  38.5 3.3 select_bitcast_fusion
  41.8 98.2 %all-gather.4.cloned.1.call-done = bf16[128,98304]{0,1:T(8,128)(2,1)} async-done(((bf16[128,12288]{0,1:T(8,128)(2,1)}), bf16[128,98304]{0,1:T(8,128)(2,1)}) %all-gather.4.cloned.1.call-update) | async-done | bytes 25165840 | tf_op jit(solution)/shard_map/all_gather | solution.py:53
  140.0 17.5 %fusion.89 = (bf16[128,12288]{0,1:T(8,128)(2,1)}, bf16[128,12288]{0,1:T(8,128)(2,1)}, bf16[128,12288]{0,1:T(8,128)(2,1)}, bf16[128,12288]{0,1:T(8,128)(2,1)}, bf...) fusion(bf16[128,98304]{0,1:T(8,128)(2,1)} %all-gather.4.cloned., ...), kind=kLoop, calls=%fused_computation.145 | loop fusion | bytes 50331648 | tf_op jit(solution)/shard_map/slice | solution.py:61
  157.5 4.7 copy.46
  162.2 4.7 copy.50
  166.8 4.7 copy.52
  171.5 4.6 copy.54
  176.1 4.7 copy.56
  180.8 4.6 copy.58
  185.4 4.7 copy.60
  190.1 4.6 copy.62
  194.8 2.5 gather_fusion.1
  197.3 1.3 fusion.38
  198.6 1.9 dynamic_update_slice.24
  200.5 3.2 gather_fusion.3
  203.7 3.2 gather_fusion.4
  207.0 3.2 gather_fusion.5
  210.2 3.2 gather_fusion.6
  213.4 3.2 gather_fusion.7
  216.6 3.2 gather_fusion.8
  219.8 2.5 gather_fusion.9
  222.4 2.3 convolution_dynamic-update-slice_fusion.6
  224.7 2.2 convolution_dynamic-update-slice_fusion.5
  226.8 2.0 convolution_dynamic-update-slice_fusion.4
  228.9 1.1 convolution_dynamic-update-slice_fusion.3
  230.0 1.1 convolution_dynamic-update-slice_fusion.2
  231.1 1.1 convolution_dynamic-update-slice_fusion.1
  232.2 1.1 convolution_dynamic-update-slice_fusion
  233.3 47.8 %reduce-scatter.3.cloned.1.call-done = bf16[18,128,128]{2,1,0:T(8,128)(2,1)} async-done(((bf16[72,128,128]{2,1,0:T(8,128)(2,1)}), bf16[18,128,128]{2,1,0:T(8,128)(2,1)}) %reduce-scatter.3.cloned.1.call-update) | async-done | bytes 589840 | tf_op jit(solution)/shard_map/reduce_scatter | solution.py:76
  281.4 32.7 %copy.64 = bf16[128,768,128]{2,0,1:T(8,128)(2,1)} copy(bf16[128,768,128]{0,2,1:T(8,128)(2,1)} %bitcast.86) | data formatting | bytes 50331648 | tf_op jit(solution)/shard_map/reshape | solution.py:16
  314.1 10.7 %gather_fusion = bf16[72,128,128]{2,1,0:T(8,128)(2,1)} fusion(bf16[128,768,128]{2,0,1:T(8,128)(2,1)} %copy.64, s32[1024]{0:T(1024)S(1)} %pad_clamp_fusion), kind=kCustom, calls=%fused_computation.10 | custom fusion | bytes 4718880 | tf_op jit(solution)/shard_map/jit(_take)/gather | solution.py:17
  324.8 2.0 fusion.27
  326.8 5.3 all-gather.6.cloned.1.call-done
  332.1 6.4 fusion.12
  338.5 6.1 copy.66
  344.6 9.0 %fusion.1 = (f32[]{:T(128)}, f32[96,128,128]{2,0,1:T(8,128)}) fusion(f32[128]{0:T(128)S(1)} %multiply_add_fusion, f32[128,72,128]{2,1,0:T(8,128)} %copy.66, s32[72]{0:T(128)S(1)} %get-tuple-element.33), kind=kOutput, calls=%fused_computation.16 | convolution fusion | flops 1363680000 | bytes 11010852 | tf_op jit(solution)/shard_map/skb,kc->scb/dot_general | solution.py:29
  353.5 39.2 %all-reduce.5 = (f32[]{:T(128)}, f32[]{:T(128)}) all-reduce(f32[]{:T(128)} %fusion.27, f32[]{:T(128)} %get-tuple-element.56), channel_id=1, replica_groups=mesh['col'=8,'row'=4] {'col','row'}, use_global_device_ids=true, to_apply=%region_2.5 | all-reduce | flops 2 | bytes 16 | tf_op jit(solution)/shard_map/psum | solution.py:83
  394.5 6.1 bitcast_multiply_fusion.1
  400.6 6.6 copy.85
  407.2 4.4 multiply_convert_fusion
  411.6 4.7 copy.68
  416.3 4.3 gather_fusion.10
  420.7 4.9 fusion.18
  425.7 47.8 %reduce-scatter.5.cloned.1.call-done = bf16[18,128,128]{2,1,0:T(8,128)(2,1)} async-done(((bf16[72,128,128]{2,1,0:T(8,128)(2,1)}), bf16[18,128,128]{2,1,0:T(8,128)(2,1)}) %reduce-scatter.5.cloned.1.call-update) | async-done | bytes 589840 | tf_op jit(solution)/shard_map/reduce_scatter | solution.py:76
  473.4 2.2 multiply_reduce_fusion
  475.6 40.0 %psum.40 = f32[]{:T(128)} all-reduce(f32[]{:T(128)} %multiply_reduce_fusion), channel_id=1, replica_groups=mesh['col'=8,'row'=4] {'col','row'}, use_global_device_ids=true, to_apply=%region_7.10 | all-reduce | flops 1 | bytes 8 | tf_op jit(solution)/shard_map/psum | solution.py:83
  516.8 3.0 fusion.26
  519.8 50.1 %all-gather.8.cloned.1.call-done = bf16[72,128,128]{2,1,0:T(8,128)(2,1)} async-done(((bf16[18,128,128]{2,1,0:T(8,128)(2,1)}), bf16[72,128,128]{2,1,0:T(8,128)(2,1)}) %all-gather.8.cloned.1.call-update) | async-done | bytes 2359312 | tf_op jit(solution)/shard_map/all_gather | solution.py:93
  570.0 6.4 fusion.15
  576.3 6.2 copy.71
  582.5 9.0 %fusion.2 = (f32[]{:T(128)}, f32[96,128,128]{2,0,1:T(8,128)}) fusion(f32[128]{0:T(128)S(1)} %multiply_add_fusion, f32[128,72,128]{2,1,0:T(8,128)} %copy.71, s32[72]{0:T(128)S(1)} %get-tuple-element.33), kind=kOutput, calls=%fused_computation.17 | convolution fusion | flops 1363680000 | bytes 11010852 | tf_op jit(solution)/shard_map/skb,kc->scb/dot_general | solution.py:29
  591.5 39.1 %all-reduce.4 = (f32[]{:T(128)}, f32[]{:T(128)}) all-reduce(f32[]{:T(128)} %get-tuple-element.58, f32[]{:T(128)} %get-tuple-element.14), channel_id=1, replica_groups=mesh['col'=8,'row'=4] {'col','row'}, use_global_device_ids=true, to_apply=%region_9.12 | all-reduce | flops 2 | bytes 16 | tf_op jit(solution)/shard_map/psum | solution.py:98
  632.5 6.1 bitcast_multiply_fusion
  638.6 6.6 copy.86
  645.2 7.7 %bitcast_subtract_fusion = f32[128,12288]{0,1:T(8,128)} fusion(f32[128,96,128]{0,2,1:T(8,128)} %copy.86, f32[128,96,128]{0,2,1:T(8,128)} %copy.85, bf16[128,12288]{0,1:T(8,128)(2,1)S(1)} %copy.47), kind=kLoop, calls=%fused_computation.18 | loop fusion | flops 4718592 | bytes 22020096 | tf_op jit(solution)/shard_map/sub | solution.py:103
  652.9 6.7 copy.73
  659.6 1.2 fusion.23
  (46 shorter events, 1.1 us)
Async XLA Ops:
  7.2 132.8 %all-gather.4.cloned.1.call-start = ((), (), s32[]{:S(2)}) async-start(), calls=%async_computation.2 | async-start | bytes 28311552 | tf_op jit(solution)/shard_map/all_gather | solution.py:53
  11.9 269.2 %reduce-scatter.3.cloned.1.call-start = ((), (), s32[]{:S(2)}) async-start(), calls=%async_computation.3 | async-start | bytes 2949120 | tf_op jit(solution)/shard_map/reduce_scatter | solution.py:76
  12.0 3.5 copy-start.6
  17.5 4.7 copy-start.9
  17.5 5.9 copy-start.7
  17.5 6.2 copy-start.8
  222.3 4.5 copy-start.1
  222.3 6.5 copy-start.4
  222.4 7.6 %copy-start.5 = (bf16[9,128,128]{2,1,0:T(8,128)(2,1)S(1)}, bf16[9,128,128]{2,1,0:T(8,128)(2,1)}, u32[]{:S(2)}) copy-start(bf16[9,128,128]{2,1,0:T(8,128)(2,1)} %gather_fusion.7) | copy-start | bytes 884740
  224.7 6.4 copy-start.3
  233.3 98.8 %all-gather.6.cloned.1.call-start = ((), (), s32[]{:S(2)}) async-start(), calls=%async_computation.4 | async-start | bytes 2949120 | tf_op jit(solution)/shard_map/all_gather | solution.py:93
  281.2 192.3 %reduce-scatter.5.cloned.1.call-start = ((), (), s32[]{:S(2)}) async-start(), calls=%async_computation.5 | async-start | bytes 2949120 | tf_op jit(solution)/shard_map/reduce_scatter | solution.py:76
  425.6 144.4 %all-gather.8.cloned.1.call-start = ((), (), s32[]{:S(2)}) async-start(), calls=%async_computation.6 | async-start | bytes 2949120 | tf_op jit(solution)/shard_map/all_gather | solution.py:93
  652.9 6.7 copy-start
  652.9 6.7 copy-start.2
Sparse Core Ops, SparseCore 0:
  12.0 127.9 all-gather.3
  233.4 47.6 reduce-scatter.2
  282.7 49.3 all-gather.5
  425.7 47.6 reduce-scatter.4
  520.0 49.9 all-gather.7
where the time goes:
time: 670 us; the launch traced here: 667 us
  waiting for transfers between devices  249 us (37%)
  local copies, waits for them, and re-layouts  184 us (27%)
  blocking collectives  128 us (19%)
  matrix products  47.8 us (7%)
  other arithmetic  38.2 us (6%)
  between operations  19.6 us (3%)
    all_gather x1, waiting for transfers between devices, on_device(): piece = lax.all_gather(samples_x, 'col', axis=1, tiled=True)  98.2 us
    reduce_scatter x2, waiting for transfers between devices, reduce_terms(): lax.psum_scatter(terms.astype(jnp.bfloat16), 'row', scatter_dimension=0,...  95.6 us
    reshape x11, local copies, waits for them, and re-layouts, take_blocks(): shaped = source.reshape(samples, source.shape[1] // BLOCK, BLOCK)  79.3 us
    psum x2, blocking collectives, norm_of(): return lax.psum(share * jnp.sum(gradient * gradient), ('col', 'row'))  79.1 us
    all_gather x2, waiting for transfers between devices, on_device(): lax.all_gather(direction, 'row', axis=0, tiled=True)  55.5 us
    gather x11, local copies, waits for them, and re-layouts, take_blocks(): return jnp.take(shaped, rows_local, axis=1)  43.6 us
    psum x1, blocking collectives, on_device(): lax.psum((jnp.sum(weight * image * image), share * jnp.sum(flat * flat)),...  39.1 us
    dot_general x2, matrix products, column_sums(): jnp.einsum('skb,kc->scb', contrib, onehot, precision=lax.Precision.HIGHEST)  17.9 us
  transfers between devices with their start and end apart: 5, of which 5 were waited for; matrix products, arithmetic and copies ran while one was open for 10% of the time, Pallas kernels for 0%

commit v1 on v0

v1 whole, which is shorter than its diff:
```python
import functools
import math

import jax
import jax.numpy as jnp
from jax import lax
from jax.experimental import pallas as pl
from jax.experimental.pallas import tpu as pltpu
from jax.sharding import PartitionSpec as P

BLOCK = 128
T_STEPS = 64
RIDGE_SHARE = 0.2
LANES = 128
VMEM = pltpu.VMEM
F32 = jnp.float32
BF16 = jnp.bfloat16
WHOLE = pl.BlockSpec(memory_space=pltpu.VMEM)
SCALARS = pl.BlockSpec(memory_space=pltpu.SMEM)


def enter(axes):
    barrier = pltpu.get_barrier_semaphore()
    count = 0
    for axis in axes:
        n = lax.axis_size(axis)
        me = lax.axis_index(axis)
        for k in range(1, n):
            pl.semaphore_signal(
                barrier, inc=1, device_id={axis: lax.rem(me + k, n)},
                device_id_type=pl.DeviceIdType.MESH,
            )
        count += n - 1
    pl.semaphore_wait(barrier, count)


def push(src, dst, send, recv, axis, k):
    n = lax.axis_size(axis)
    return pltpu.make_async_remote_copy(
        src_ref=src, dst_ref=dst, send_sem=send, recv_sem=recv,
        device_id={axis: lax.rem(lax.axis_index(axis) + k, n)},
        device_id_type=pl.DeviceIdType.MESH,
    )


def gather_small_kernel(x_ref, out_ref, send_c, recv_c, send_r, recv_r):
    cols, rows = lax.axis_size("col"), lax.axis_size("row")
    my_col, my_row = lax.axis_index("col"), lax.axis_index("row")
    enter(("col", "row"))
    out_ref[my_row, my_col] = x_ref[...]
    first = [
        push(x_ref, out_ref.at[my_row, my_col], send_c.at[k - 1], recv_c.at[k - 1], "col", k)
        for k in range(1, cols)
    ]
    for copy in first:
        copy.start()
    for copy in first:
        copy.wait()
    second = [
        push(out_ref.at[my_row], out_ref.at[my_row], send_r.at[k - 1], recv_r.at[k - 1], "row", k)
        for k in range(1, rows)
    ]
    for copy in second:
        copy.start()
    for copy in second:
        copy.wait()


def gather_small(x, call_id):
    cols, rows = lax.axis_size("col"), lax.axis_size("row")
    return pl.pallas_call(
        gather_small_kernel,
        out_shape=jax.ShapeDtypeStruct((rows, cols) + x.shape, x.dtype),
        in_specs=[WHOLE],
        out_specs=WHOLE,
        scratch_shapes=[
            pltpu.SemaphoreType.DMA((cols - 1,)), pltpu.SemaphoreType.DMA((cols - 1,)),
            pltpu.SemaphoreType.DMA((rows - 1,)), pltpu.SemaphoreType.DMA((rows - 1,)),
        ],
        compiler_params=pltpu.CompilerParams(collective_id=call_id, has_side_effects=True),
    )(x)


def select_kernel(run, index_ref, x_ref, out_ref):
    def one(b, carry):
        column = pl.multiple_of(index_ref[b] * BLOCK, BLOCK)
        out_ref[b] = x_ref[:, pl.ds(column, BLOCK)]
        return carry

    lax.fori_loop(0, out_ref.shape[0], one, 0, unroll=2)


def select_blocks(index, x):
    count = index.shape[0]
    return pl.pallas_call(
        functools.partial(select_kernel, count),
        out_shape=jax.ShapeDtypeStruct((count, x.shape[0], BLOCK), x.dtype),
        in_specs=[SCALARS, WHOLE],
        out_specs=WHOLE,
    )(index, x)


def exchange_kernel(run, x_ref, out_ref, send, recv):
    n, me = lax.axis_size("col"), lax.axis_index("col")
    enter(("col",))
    copies = []
    for k in range(1, n):
        peer = lax.rem(me + k, n)
        copies.append(
            push(x_ref.at[pl.ds(peer * run, run)], out_ref.at[pl.ds(me * run, run)],
                 send.at[k - 1], recv.at[k - 1], "col", k)
        )
    for copy in copies:
        copy.start()

    def own(i, carry):
        out_ref[me * run + i] = x_ref[me * run + i]
        return carry

    lax.fori_loop(0, run, own, 0)
    for copy in copies:
        copy.wait()


def exchange_blocks(x, call_id):
    n = lax.axis_size("col")
    return pl.pallas_call(
        functools.partial(exchange_kernel, x.shape[0] // n),
        out_shape=jax.ShapeDtypeStruct(x.shape, x.dtype),
        in_specs=[WHOLE],
        out_specs=WHOLE,
        scratch_shapes=[pltpu.SemaphoreType.DMA((n - 1,)), pltpu.SemaphoreType.DMA((n - 1,))],
        compiler_params=pltpu.CompilerParams(collective_id=call_id, has_side_effects=True),
    )(x)


def block_dot(x, e):
    return lax.dot_general(x, e, (((0,), (0,)), ((), ())), preferred_element_type=F32)


def unroll_of(count):
    return math.gcd(count, 4)


def first_terms_kernel(cols_ref, x_ref, t_ref, w_ref, out_ref):
    count = x_ref.shape[0]
    step = unroll_of(count)

    def some(i, carry):
        for j in range(step):
            b = i * step + j
            place = pl.ds(pl.multiple_of(cols_ref[b] * BLOCK, BLOCK), BLOCK)
            e = (t_ref[:, place].astype(F32) * w_ref[...]).astype(BF16)
            out_ref[b] = block_dot(x_ref[b], e).astype(BF16)
        return carry

    lax.fori_loop(0, count // step, some, 0)


def first_terms(cols, x, targets, weight):
    return pl.pallas_call(
        first_terms_kernel,
        out_shape=jax.ShapeDtypeStruct((x.shape[0], BLOCK, BLOCK), BF16),
        in_specs=[SCALARS, WHOLE, WHOLE, WHOLE],
        out_specs=WHOLE,
    )(cols, x, targets, weight)


def next_terms_kernel(cols_ref, scale_ref, x_ref, t_ref, image_ref, w_ref, out_ref):
    count = x_ref.shape[0]
    step = unroll_of(count)
    alpha = scale_ref[0]

    def some(i, carry):
        for j in range(step):
            b = i * step + j
            place = pl.ds(pl.multiple_of(cols_ref[b] * BLOCK, BLOCK), BLOCK)
            left = t_ref[:, place].astype(F32) - alpha * image_ref[:, place]
            out_ref[b] = block_dot(x_ref[b], (left * w_ref[...]).astype(BF16)).astype(BF16)
        return carry

    lax.fori_loop(0, count // step, some, 0)


def next_terms(cols, scale, x, targets, image, weight):
    return pl.pallas_call(
        next_terms_kernel,
        out_shape=jax.ShapeDtypeStruct((x.shape[0], BLOCK, BLOCK), BF16),
        in_specs=[SCALARS, SCALARS, WHOLE, WHOLE, WHOLE, WHOLE],
        out_specs=WHOLE,
    )(cols, scale, x, targets, image, weight)


def reduce_gather_kernel(pieces, first, *refs):
    if first:
        terms_ref, out_ref, own_ref, sums_ref, held, rs_send, rs_recv, ag_send, ag_recv = refs
        before_ref = None
        shift = None
    else:
        (scale_ref, terms_ref, before_ref, out_ref, own_ref, sums_ref, held,
         rs_send, rs_recv, ag_send, ag_recv) = refs
        shift = scale_ref[1]
    n, me = lax.axis_size("row"), lax.axis_index("row")
    share = own_ref.shape[0]
    size = share // pieces
    enter(("row",))
    scatter, spread = [], []
    for p in range(pieces):
        part = []
        for k in range(1, n):
            peer = lax.rem(me + k, n)
            part.append(
                push(terms_ref.at[pl.ds(peer * share + p * size, size)],
                     held.at[k - 1, pl.ds(p * size, size)],
                     rs_send.at[p, k - 1], rs_recv.at[p, k - 1], "row", k)
            )
        for copy in part:
            copy.start()
        scatter.append(part)
    sums_ref[...] = jnp.zeros_like(sums_ref)
    for p in range(pieces):
        for copy in scatter[p]:
            copy.wait_recv()

        def one(i, carry):
            total = terms_ref[me * share + i].astype(F32)
            for k in range(1, n):
                total = total + held[k - 1, i].astype(F32)
            if before_ref is not None:
                flat = before_ref[i].astype(F32)
                total = total - shift * flat
            rounded = total.astype(BF16)
            own_ref[i] = rounded
            out_ref[me * share + i] = rounded
            wide = rounded.astype(F32)
            sums_ref[0:1, :] += jnp.sum(total * total, axis=0, keepdims=True)
            sums_ref[1:2, :] += jnp.sum(wide * wide, axis=0, keepdims=True)
            if before_ref is not None:
                sums_ref[2:3, :] += jnp.sum(wide * flat, axis=0, keepdims=True)
            return carry

        lax.fori_loop(p * size, (p + 1) * size, one, 0)
        part = [
            push(own_ref.at[pl.ds(p * size, size)],
                 out_ref.at[pl.ds(me * share + p * size, size)],
                 ag_send.at[p, k - 1], ag_recv.at[p, k - 1], "row", k)
            for k in range(1, n)
        ]
        for copy in part:
            copy.start()
        spread.append(part)
    for part in scatter:
        for copy in part:
            copy.wait_send()
    for part in spread:
        for copy in part:
            copy.wait()


def reduce_gather(terms, scale, before, call_id):
    n = lax.axis_size("row")
    share = terms.shape[0] // n
    pieces = math.gcd(share, 3)
    first = before is None
    sems = pltpu.SemaphoreType.DMA((pieces, n - 1))
    return pl.pallas_call(
        functools.partial(reduce_gather_kernel, pieces, first),
        out_shape=(
            jax.ShapeDtypeStruct(terms.shape, BF16),
            jax.ShapeDtypeStruct((share, BLOCK, BLOCK), BF16),
            jax.ShapeDtypeStruct((8, LANES), F32),
        ),
        in_specs=[WHOLE] if first else [SCALARS, WHOLE, WHOLE],
        out_specs=(WHOLE, WHOLE, WHOLE),
        scratch_shapes=[VMEM((n - 1, share, BLOCK, BLOCK), BF16), sems, sems, sems, sems],
        compiler_params=pltpu.CompilerParams(collective_id=call_id, has_side_effects=True),
    )(*((terms,) if first else (scale, terms, before)))


def apply_kernel(first, cols_ref, x_ref, d_ref, w_ref, *refs):
    if first:
        image_ref, sums_ref = refs
        before_ref = None
    else:
        before_ref, image_ref, sums_ref = refs
    count = x_ref.shape[0]
    step = unroll_of(count)
    columns = image_ref.shape[1] // BLOCK
    samples = image_ref.shape[0]

    def clear(i, carry):
        place = pl.ds(pl.multiple_of(i * BLOCK, BLOCK), BLOCK)
        image_ref[:, place] = jnp.zeros((samples, BLOCK), F32)
        return carry

    lax.fori_loop(0, columns, clear, 0, unroll=2)

    def some(i, carry):
        made = [
            jnp.dot(x_ref[i * step + j], d_ref[i * step + j], preferred_element_type=F32)
            for j in range(step)
        ]
        for j in range(step):
            place = pl.ds(pl.multiple_of(cols_ref[i * step + j] * BLOCK, BLOCK), BLOCK)
            image_ref[:, place] += made[j]
        return carry

    lax.fori_loop(0, count // step, some, 0)
    sums_ref[...] = jnp.zeros_like(sums_ref)

    def measure(i, carry):
        place = pl.ds(pl.multiple_of(i * BLOCK, BLOCK), BLOCK)
        image = image_ref[:, place]
        weighted = w_ref[...] * image
        sums_ref[0:1, :] += jnp.sum(weighted * image, axis=0, keepdims=True)
        if before_ref is not None:
            sums_ref[1:2, :] += jnp.sum(weighted * before_ref[:, place], axis=0, keepdims=True)
        return carry

    lax.fori_loop(0, columns, measure, 0, unroll=2)


def apply_blocks(cols, x, direction, weight, before, taxa):
    first = before is None
    samples = x.shape[1]
    return pl.pallas_call(
        functools.partial(apply_kernel, first),
        out_shape=(
            jax.ShapeDtypeStruct((samples, taxa), F32),
            jax.ShapeDtypeStruct((8, LANES), F32),
        ),
        in_specs=[SCALARS] + [WHOLE] * (3 if first else 4),
        out_specs=(WHOLE, WHOLE),
    )(cols, x, direction, weight, *(() if first else (before,)))


def on_device(samples_x, targets, times, block_rows, block_cols):
    col_count = lax.axis_size("col")
    row_count = lax.axis_size("row")
    taxa_col = samples_x.shape[1]
    sample_count = samples_x.shape[0]
    column_count = taxa_col // BLOCK
    my_col = lax.axis_index("col")
    my_row = lax.axis_index("row")
    shard = block_rows.shape[0]
    group_count = shard * row_count
    run = group_count // col_count
    ridge = RIDGE_SHARE * sample_count * row_count
    weight = jnp.broadcast_to(
        (0.5 + times.astype(F32) / T_STEPS)[:, None], (sample_count, BLOCK)
    )
    places = jnp.pad(
        jnp.stack([block_rows, block_cols]), ((0, 6), (0, LANES - shard))
    )
    everywhere = gather_small(places, 1)
    rows_all = everywhere[:, :, 0, :shard].transpose(1, 0, 2).reshape(col_count, group_count)
    wanted = lax.dynamic_slice_in_dim(rows_all, my_col * run, run, 1) - my_col * column_count
    cols_mine = lax.dynamic_index_in_dim(everywhere[:, :, 1, :shard], my_col, 1, keepdims=False)
    cols = cols_mine.reshape(group_count) - my_col * column_count

    x = exchange_blocks(select_blocks(wanted.reshape(-1), samples_x), 2)
    terms = first_terms(cols, x, targets, weight)
    direction, own0, sums0 = reduce_gather(terms, None, None, 3)
    image0, norms0 = apply_blocks(cols, x, direction, weight, None, taxa_col)
    totals = jnp.sum(
        gather_small(jnp.concatenate([sums0[:2], norms0[:1], jnp.zeros((5, LANES), F32)]), 4),
        axis=(0, 1, 3),
    )
    gamma, flat_norm, image_norm = totals[0], totals[1], totals[2]
    alpha0 = gamma / (image_norm + ridge * flat_norm)
    scale = jnp.stack([alpha0, ridge * alpha0])
    terms = next_terms(cols, scale, x, targets, image0, weight)
    spread, own1, sums1 = reduce_gather(terms, scale, own0, 5)
    image1, norms1 = apply_blocks(cols, x, spread, weight, image0, taxa_col)
    totals = jnp.sum(
        gather_small(jnp.concatenate([sums1[:3], norms1[:2], jnp.zeros((3, LANES), F32)]), 6),
        axis=(0, 1, 3),
    )
    beta = totals[0] / gamma
    flat_next = totals[1] + 2.0 * beta * totals[2] + beta * beta * flat_norm
    image_next = totals[3] + 2.0 * beta * totals[4] + beta * beta * image_norm
    alpha1 = totals[0] / (image_next + ridge * flat_next)
    mixed = alpha0 + alpha1 * beta
    coeffs = mixed * own0.astype(F32) + alpha1 * own1.astype(F32)
    residual = targets.astype(F32) - mixed * image0 - alpha1 * image1
    return (coeffs, residual)


def solution(mesh):
    placed = (P("row", "col"), P("row", "col"), P("row"), P(("col", "row")), P(("col", "row")))
    return jax.shard_map(
        on_device,
        mesh=mesh,
        in_specs=placed,
        out_specs=(P(("col", "row"), None, None), P("row", "col")),
        check_vma=False,
    )
```

time: 670 us -> 364 us (0.54)
  Pallas kernels: 0 us -> 331 us
  waiting for transfers between devices: 249 us -> 0 us
  local copies, waits for them, and re-layouts: 184 us -> 7.9 us
  blocking collectives: 128 us -> 0 us
  matrix products: 47.8 us -> 0 us
  other arithmetic: 38.2 us -> 15.3 us
  between operations: 19.6 us -> 8.31 us
    pallas_call x0 -> x11, Pallas kernels: none -> 331 us  [the longest x2 209 us: reduce_gather(): pl.pallas_call(functools.partial(reduce_gather_kernel, pieces, first), ou...]
    all_gather x3 -> x0, waiting for transfers between devices: 154 us -> none  [the longest x1 98.2 us: on_device(): piece = lax.all_gather(samples_x, 'col', axis=1, tiled=True)]
    psum x3 -> x0, blocking collectives: 118 us -> none  [the longest x2 79.1 us: norm_of(): return lax.psum(share * jnp.sum(gradient * gradient), ('col', 'row'))]
    reduce_scatter x2 -> x0, waiting for transfers between devices: 95.6 us -> none  [reduce_terms(): lax.psum_scatter(terms.astype(jnp.bfloat16), 'row', scatter_dimension=0,...]
    reshape x11 -> x2, local copies, waits for them, and re-layouts: 79.3 us -> 0.7 us  [the longest x1 0.62 us: on_device(): x = exchange_blocks(select_blocks(wanted.reshape(-1), samples_x), 2)]
    dot_general x13 -> x0, matrix products: 47.8 us -> none  [the longest x2 17.9 us: column_sums(): jnp.einsum('skb,kc->scb', contrib, onehot, precision=lax.Precision.HIGHEST)]
    gather x11 -> x0, local copies, waits for them, and re-layouts: 43.6 us -> none  [take_blocks(): return jnp.take(shaped, rows_local, axis=1)]
    unnamed x28 -> x6, local copies, waits for them, and re-layouts: 15.9 us -> 0.01 us
  transfers between devices with their start and end apart: 5 -> 0, of which waited for: 5 -> 0; matrix products, arithmetic and copies ran while one was open for 10% -> 0% of each run, Pallas kernels for 0% -> 0%
where the time goes in v1:
time: 364 us; the launch traced here: 363 us
  Pallas kernels  331 us (91%)
  other arithmetic  15.3 us (4%)
  between operations  8.31 us (2%)
  local copies, waits for them, and re-layouts  7.9 us (2%)
    pallas_call x2, Pallas kernels, reduce_gather(): pl.pallas_call(functools.partial(reduce_gather_kernel, pieces, first), ou...  209 us
    pallas_call x3, Pallas kernels, gather_small(): pl.pallas_call(gather_small_kernel, out_shape=jax.ShapeDtypeStruct((rows,...  44.7 us
    pallas_call x1, Pallas kernels, exchange_blocks(): pl.pallas_call(functools.partial(exchange_kernel, x.shape[0] // n), out_s...  30.4 us
    pallas_call x2, Pallas kernels, apply_blocks(): pl.pallas_call(functools.partial(apply_kernel, first), out_shape=(jax.Sha...  24.7 us
    pallas_call x1, Pallas kernels, next_terms(): pl.pallas_call(next_terms_kernel, out_shape=jax.ShapeDtypeStruct((x.shape...  9.99 us
    sub x1, other arithmetic, on_device(): residual = targets.astype(F32) - mixed * image0 - alpha1 * image1  8.61 us
    pallas_call x1, Pallas kernels, first_terms(): pl.pallas_call(first_terms_kernel, out_shape=jax.ShapeDtypeStruct((x.shap...  7.93 us

profile of v1, /device:TPU:0, one launch (start us, length us, event | category | flops | bytes accessed | tf_op | source)
XLA Modules:
  0.0 362.9 jit_solution(624819802521439954)
XLA Ops:
  0.6 0.7 multiply_add_fusion.1
  1.3 0.1 pad.7.clone
  1.4 0.1 pad.12.clone
  1.5 0.7 pad_add_fusion
  2.1 0.6 pad.4.x_ref
  2.7 0.7 broadcast_in_dim.12.w_ref
  3.4 14.4 %shard_map.68 = s32[4,8,8,128]{3,2,1,0:T(8,128)} custom-call(s32[8,128]{1,0:T(8,128)} %pad.4.x_ref), custom_call_target="tpu_custom_call" | custom-call | tf_op jit(solution)/shard_map/pallas_call | solution.py:71
  17.9 1.0 fusion
  18.9 0.1 reshape.17
  19.0 0.1 dynamic-slice_subtract_fusion
  19.1 0.6 reshape.18.index_ref
  19.7 0.7 sub.22.cols_ref
  20.4 4.1 %shard_map.69.x_ref = bf16[72,128,128]{2,1,0:T(8,128)(2,1)} custom-call(s32[72]{0:T(128)} %reshape.18.index_ref, bf16[128,12288]{1,0:T(8,128)(2,1)} %x_ref.1), custom_call_target="tpu_custom_call" | custom-call | tf_op jit(solution)/shard_map/pallas_call | solution.py:95
  24.5 30.4 %shard_map.70.x_ref = bf16[72,128,128]{2,1,0:T(8,128)(2,1)} custom-call(bf16[72,128,128]{2,1,0:T(8,128)(2,1)} %shard_map.69.x_ref), custom_call_target="tpu_custom_call" | custom-call | tf_op jit(solution)/shard_map/pallas_call | solution.py:127
  55.0 7.9 %shard_map.71.refs_0_ = bf16[72,128,128]{2,1,0:T(8,128)(2,1)} custom-call(s32[72]{0:T(128)} %sub.22.cols_ref, bf16[72,128,128]{2,1,0:T(8,128)(2,1)} %shard_map.70.x_ref, bf16[128,12288]{1,0:T(8,128)(2,1)} %t_ref.3, f32[128,128]{1,0:T(8,128)} %broadcast_in_dim.12.w_ref), custom_call_target="tpu_custom_call" | custom-call | tf_op jit(solution)/shard_map/pallas_call | solution.py:161
  62.9 104.5 %shard_map.72 = (bf16[72,128,128]{2,1,0:T(8,128)(2,1)}, bf16[18,128,128]{2,1,0:T(8,128)(2,1)}, f32[8,128]{1,0:T(8,128)}) custom-call(bf16[72,128,128]{2,1,0:T(8,128)(2,1)} %shard_map.71.refs_0_), custom_call_target="tpu_custom_call" | custom-call | tf_op jit(solution)/shard_map/pallas_call | solution.py:266
  167.4 0.7 slice.45
  168.1 11.0 %shard_map.73 = (f32[128,12288]{1,0:T(8,128)}, f32[8,128]{1,0:T(8,128)}) custom-call(s32[72]{0:T(128)} %sub.22.cols_ref, bf16[72,128,128]{2,1,0:T(8,128)(2,1)} %shard_map.70.x_ref, bf16[72,128,128]{2,1,0:T(8,128)(2,1)} %get-tuple-element.13.d_ref, f32[128,128]{1,0:T(8,128)} %broadcast_in_dim.12.w_ref), custom_call_target="tpu_custom_call" | custom-call | tf_op jit(solution)/shard_map/pallas_call | solution.py:326
  179.1 0.7 slice.46
  179.8 0.7 maximum_maximum_fusion.x_ref
  180.4 16.4 %shard_map.74 = f32[4,8,8,128]{3,2,1,0:T(8,128)} custom-call(f32[8,128]{1,0:T(8,128)} %maximum_maximum_fusion.x_ref), custom_call_target="tpu_custom_call" | custom-call | tf_op jit(solution)/shard_map/pallas_call | solution.py:71
  196.8 1.1 reduce_sum.18
  197.8 0.6 fusion.2
  200.3 0.6 pad_maximum_fusion.scale_ref.refs_0_
  201.0 10.0 %shard_map.75.refs_1_ = bf16[72,128,128]{2,1,0:T(8,128)(2,1)} custom-call(s32[72]{0:T(128)} %sub.22.cols_ref, f32[2]{0:T(128)} %pad_maximum_fusion.scale_ref.refs_0_, bf16[72,128,128]{2,1,0:T(8,128)(2,1)} %shard_map.70.x_ref, bf16[128,12288]{1,0:T(8,128)(2,1)} %t_ref.3, f32[128,12288]{1,0:T(8,128)} %get-tuple-element.15.image_ref.refs_0_, ...), custom_call_target="tpu_custom_call" | custom-call | tf_op jit(solution)/shard_map/pallas_call | solution.py:186
  211.0 105.0 %shard_map.76 = (bf16[72,128,128]{2,1,0:T(8,128)(2,1)}, bf16[18,128,128]{2,1,0:T(8,128)(2,1)}, f32[8,128]{1,0:T(8,128)}) custom-call(f32[2]{0:T(128)} %pad_maximum_fusion.scale_ref.refs_0_, bf16[72,128,128]{2,1,0:T(8,128)(2,1)} %shard_map.75.refs_1_, bf16[18,128,128]{2,1,0:T(8,128)(2,1)} %get-tuple-element.16.refs_2_), custom_call_target="tpu_custom_call" | custom-call | tf_op jit(solution)/shard_map/pallas_call | solution.py:266
  316.0 0.7 slice.50
  316.6 0.0 copy-start
  316.6 13.7 %shard_map.77 = (f32[128,12288]{1,0:T(8,128)}, f32[8,128]{1,0:T(8,128)}) custom-call(s32[72]{0:T(128)} %sub.22.cols_ref, bf16[72,128,128]{2,1,0:T(8,128)(2,1)} %shard_map.70.x_ref, bf16[72,128,128]{2,1,0:T(8,128)(2,1)} %get-tuple-element.18.d_ref, f32[128,128]{1,0:T(8,128)} %broadcast_in_dim.12.w_ref, f32[128,12288]{1,0:T(8,128)} %get-tuple-element.15.image_ref.refs_0_), custom_call_target="tpu_custom_call" | custom-call | tf_op jit(solution)/shard_map/pallas_call | solution.py:326
  330.3 0.7 slice.51
  331.0 0.7 maximum_maximum_fusion.1.x_ref
  331.6 13.9 %shard_map.78 = f32[4,8,8,128]{3,2,1,0:T(8,128)} custom-call(f32[8,128]{1,0:T(8,128)} %maximum_maximum_fusion.1.x_ref), custom_call_target="tpu_custom_call" | custom-call | tf_op jit(solution)/shard_map/pallas_call | solution.py:71
  345.6 1.1 reduce_sum.19
  346.6 0.7 fusion.1
  353.1 0.0 copy-done
  353.1 0.0 copy-start.1
  353.1 0.0 copy-start.2
  353.1 8.6 %multiply_subtract_fusion = f32[128,12288]{1,0:T(8,128)} fusion(f32[128,12288]{1,0:T(8,128)} %get-tuple-element.21, f32[128,12288]{1,0:T(8,128)} %get-tuple-element.15.image_ref.refs_0_, bf16[128,12288]{1,0:T(8,128)(2,1)S(1)} %copy-done, f32[]{:T(128)S(6)} %div.19, f32[]{:T(128)S(6)} %add.49), kind=kLoop, calls=%fused_computation | loop fusion | flops 7864320 | bytes 22020104 | tf_op jit(solution)/shard_map/sub | solution.py:385
  361.7 0.0 copy-done.1
  361.7 0.0 copy-done.2
  361.7 1.2 multiply_add_fusion
  (4 shorter events, 0.0 us)
Async XLA Ops:
  316.6 36.4 %copy-start = (bf16[128,12288]{1,0:T(8,128)(2,1)S(1)}, bf16[128,12288]{1,0:T(8,128)(2,1)}, u32[]{:S(2)}) copy-start(bf16[128,12288]{1,0:T(8,128)(2,1)} %t_ref.3) | copy-start | bytes 9437188
  353.1 8.6 %copy-start.1 = (bf16[18,128,128]{2,1,0:T(8,128)(2,1)S(1)}, bf16[18,128,128]{2,1,0:T(8,128)(2,1)}, u32[]{:S(2)}) copy-start(bf16[18,128,128]{2,1,0:T(8,128)(2,1)} %get-tuple-element.16.refs_2_) | copy-start | bytes 1769476
  353.1 8.6 %copy-start.2 = (bf16[18,128,128]{2,1,0:T(8,128)(2,1)S(1)}, bf16[18,128,128]{2,1,0:T(8,128)(2,1)}, u32[]{:S(2)}) copy-start(bf16[18,128,128]{2,1,0:T(8,128)(2,1)} %get-tuple-element.20) | copy-start | bytes 1769476

commit v2 on v1

--- a/solution.py
+++ b/solution.py
@@ -191,80 +191,140 @@
     )(cols, scale, x, targets, image, weight)
 
 
-def reduce_gather_kernel(pieces, first, *refs):
+def sweep_kernel(first, *refs):
     if first:
-        terms_ref, out_ref, own_ref, sums_ref, held, rs_send, rs_recv, ag_send, ag_recv = refs
+        (terms_ref, out_ref, own_ref, sums_ref, from_left, from_right, to_right, to_left,
+         send_r, recv_r, send_l, recv_l) = refs
         before_ref = None
-        shift = None
     else:
-        (scale_ref, terms_ref, before_ref, out_ref, own_ref, sums_ref, held,
-         rs_send, rs_recv, ag_send, ag_recv) = refs
+        (scale_ref, terms_ref, before_ref, out_ref, own_ref, sums_ref, from_left, from_right,
+         to_right, to_left, send_r, recv_r, send_l, recv_l) = refs
         shift = scale_ref[1]
     n, me = lax.axis_size("row"), lax.axis_index("row")
+    pieces = send_r.shape[0]
+    size = terms_ref.shape[0] // pieces
     share = own_ref.shape[0]
-    size = share // pieces
-    enter(("row",))
-    scatter, spread = [], []
-    for p in range(pieces):
-        part = []
-        for k in range(1, n):
-            peer = lax.rem(me + k, n)
-            part.append(
-                push(terms_ref.at[pl.ds(peer * share + p * size, size)],
-                     held.at[k - 1, pl.ds(p * size, size)],
-                     rs_send.at[p, k - 1], rs_recv.at[p, k - 1], "row", k)
-            )
-        for copy in part:
-            copy.start()
-        scatter.append(part)
+    has_left, has_right = me > 0, me < n - 1
+    barrier = pltpu.get_barrier_semaphore()
+
+    def greet(k):
+        pl.semaphore_signal(
+            barrier, inc=1, device_id={"row": lax.rem(me + k, n)},
+            device_id_type=pl.DeviceIdType.MESH,
+        )
+
+    pl.when(has_left)(lambda: greet(n - 1))
+    pl.when(has_right)(lambda: greet(1))
+    pl.semaphore_wait(barrier, has_left.astype(jnp.int32) + has_right.astype(jnp.int32))
+
+    def rightward(src, p):
+        place = pl.ds(p * size, size)
+        return push(src.at[place], from_left.at[place], send_r.at[p], recv_r.at[p], "row", 1)
+
+    def leftward(src, p):
+        place = pl.ds(p * size, size)
+        return push(src.at[place], from_right.at[place], send_l.at[p], recv_l.at[p], "row", n - 1)
+
+    def begin(source, heading):
+        def one(p, carry):
+            heading(source, p).start()
+            return carry
+
+        lax.fori_loop(0, pieces, one, 0)
+
+    def clear(buffer):
+        def one(i, carry):
+            buffer[i] = jnp.zeros((BLOCK, BLOCK), BF16)
+            return carry
+
+        lax.fori_loop(0, buffer.shape[0], one, 0)
+
+    @pl.when(me == 0)
+    def _():
+        begin(terms_ref, rightward)
+        clear(from_left)
+
+    @pl.when(me == n - 1)
+    def _():
+        begin(terms_ref, leftward)
+        clear(from_right)
+
+    def add(arrived, staged, p):
+        def one(i, carry):
+            b = p * size + i
+            staged[b] = (arrived[b].astype(F32) + terms_ref[b].astype(F32)).astype(BF16)
+            return carry
+
+        lax.fori_loop(0, size, one, 0)
+
+    def total_of(b):
+        total = terms_ref[b].astype(F32) + from_left[b].astype(F32) + from_right[b].astype(F32)
+        if before_ref is not None:
+            total = total - shift * before_ref[b].astype(F32)
+        return total
+
+    def piece(p, carry):
+        @pl.when(has_left)
+        def _():
+            rightward(to_right, p).wait_recv()
+
+            @pl.when(has_right)
+            def _():
+                add(from_left, to_right, p)
+                rightward(to_right, p).start()
+
+        @pl.when(has_right)
+        def _():
+            leftward(to_left, p).wait_recv()
+
+            @pl.when(has_left)
+            def _():
+                add(from_right, to_left, p)
+                leftward(to_left, p).start()
+
+        def one(i, inner):
+            b = p * size + i
+            out_ref[b] = total_of(b).astype(BF16)
+            return inner
+
+        lax.fori_loop(0, size, one, 0)
+        return carry
+
+    lax.fori_loop(0, pieces, piece, 0)
     sums_ref[...] = jnp.zeros_like(sums_ref)
-    for p in range(pieces):
-        for copy in scatter[p]:
-            copy.wait_recv()
-
-        def one(i, carry):
-            total = terms_ref[me * share + i].astype(F32)
-            for k in range(1, n):
-                total = total + held[k - 1, i].astype(F32)
-            if before_ref is not None:
-                flat = before_ref[i].astype(F32)
-                total = total - shift * flat
-            rounded = total.astype(BF16)
-            own_ref[i] = rounded
-            out_ref[me * share + i] = rounded
-            wide = rounded.astype(F32)
-            sums_ref[0:1, :] += jnp.sum(total * total, axis=0, keepdims=True)
-            sums_ref[1:2, :] += jnp.sum(wide * wide, axis=0, keepdims=True)
-            if before_ref is not None:
-                sums_ref[2:3, :] += jnp.sum(wide * flat, axis=0, keepdims=True)
-            return carry
-
-        lax.fori_loop(p * size, (p + 1) * size, one, 0)
-        part = [
-            push(own_ref.at[pl.ds(p * size, size)],
-                 out_ref.at[pl.ds(me * share + p * size, size)],
-                 ag_send.at[p, k - 1], ag_recv.at[p, k - 1], "row", k)
-            for k in range(1, n)
-        ]
-        for copy in part:
-            copy.start()
-        spread.append(part)
-    for part in scatter:
-        for copy in part:
-            copy.wait_send()
-    for part in spread:
-        for copy in part:
-            copy.wait()
-
-
-def reduce_gather(terms, scale, before, call_id):
+
+    def own(i, carry):
+        b = me * share + i
+        total = total_of(b)
+        rounded = total.astype(BF16)
+        own_ref[i] = rounded
+        wide = rounded.astype(F32)
+        sums_ref[0:1, :] += jnp.sum(total * total, axis=0, keepdims=True)
+        sums_ref[1:2, :] += jnp.sum(wide * wide, axis=0, keepdims=True)
+        if before_ref is not None:
+            flat = before_ref[b].astype(F32)
+            sums_ref[2:3, :] += jnp.sum(wide * flat, axis=0, keepdims=True)
+        return carry
+
+    lax.fori_loop(0, share, own, 0)
+
+    def finish(p, carry):
+        pl.when(has_right)(lambda: rightward(to_right, p).wait_send())
+        pl.when(has_left)(lambda: leftward(to_left, p).wait_send())
+        return carry
+
+    lax.fori_loop(0, pieces, finish, 0)
+
+
+def sweep(terms, scale, before, call_id):
     n = lax.axis_size("row")
     share = terms.shape[0] // n
-    pieces = math.gcd(share, 3)
+    pieces = math.gcd(terms.shape[0], 12)
     first = before is None
-    sems = pltpu.SemaphoreType.DMA((pieces, n - 1))
-    return pl.pallas_call(
-        functools.partial(reduce_gather_kernel, pieces, first),
+    sems = pltpu.SemaphoreType.DMA((pieces,))
+    whole = VMEM(terms.shape, BF16)
+    return pl.pallas_call(
+        functools.partial(sweep_kernel, first),
         out_shape=(
             jax.ShapeDtypeStruct(terms.shape, BF16),
             jax.ShapeDtypeStruct((share, BLOCK, BLOCK), BF16),
@@ -272,7 +332,7 @@
         ),
         in_specs=[WHOLE] if first else [SCALARS, WHOLE, WHOLE],
         out_specs=(WHOLE, WHOLE, WHOLE),
-        scratch_shapes=[VMEM((n - 1, share, BLOCK, BLOCK), BF16), sems, sems, sems, sems],
+        scratch_shapes=[whole, whole, whole, whole, sems, sems, sems, sems],
         compiler_params=pltpu.CompilerParams(collective_id=call_id, has_side_effects=True),
     )(*((terms,) if first else (scale, terms, before)))
 
@@ -341,7 +401,6 @@
     sample_count = samples_x.shape[0]
     column_count = taxa_col // BLOCK
     my_col = lax.axis_index("col")
-    my_row = lax.axis_index("row")
     shard = block_rows.shape[0]
     group_count = shard * row_count
     run = group_count // col_count
@@ -360,7 +419,7 @@
 
     x = exchange_blocks(select_blocks(wanted.reshape(-1), samples_x), 2)
     terms = first_terms(cols, x, targets, weight)
-    direction, own0, sums0 = reduce_gather(terms, None, None, 3)
+    direction, own0, sums0 = sweep(terms, None, None, 3)
     image0, norms0 = apply_blocks(cols, x, direction, weight, None, taxa_col)
     totals = jnp.sum(
         gather_small(jnp.concatenate([sums0[:2], norms0[:1], jnp.zeros((5, LANES), F32)]), 4),
@@ -370,7 +429,7 @@
     alpha0 = gamma / (image_norm + ridge * flat_norm)
     scale = jnp.stack([alpha0, ridge * alpha0])
     terms = next_terms(cols, scale, x, targets, image0, weight)
-    spread, own1, sums1 = reduce_gather(terms, scale, own0, 5)
+    spread, own1, sums1 = sweep(terms, scale, direction, 5)
     image1, norms1 = apply_blocks(cols, x, spread, weight, image0, taxa_col)
     totals = jnp.sum(
         gather_small(jnp.concatenate([sums1[:3], norms1[:2], jnp.zeros((3, LANES), F32)]), 6),

time: 364 us -> 439 us (1.21)
  Pallas kernels: 331 us -> 407 us
    pallas_call x2, Pallas kernels: 209 us -> 292 us  [sweep(): pl.pallas_call(functools.partial(sweep_kernel, first), out_shape=(jax.Sha...]
    pallas_call x3, Pallas kernels: 44.7 us -> 38.5 us  [gather_small(): pl.pallas_call(gather_small_kernel, out_shape=jax.ShapeDtypeStruct((rows,...]
where the time goes in v2:
time: 439 us
  Pallas kernels  407 us (93%)
  other arithmetic  15.3 us (3%)
  between operations  8.3 us (2%)
  local copies, waits for them, and re-layouts  7.86 us (2%)
    pallas_call x2, Pallas kernels, sweep(): pl.pallas_call(functools.partial(sweep_kernel, first), out_shape=(jax.Sha...  292 us
    pallas_call x3, Pallas kernels, gather_small(): pl.pallas_call(gather_small_kernel, out_shape=jax.ShapeDtypeStruct((rows,...  38.5 us
    pallas_call x1, Pallas kernels, exchange_blocks(): pl.pallas_call(functools.partial(exchange_kernel, x.shape[0] // n), out_s...  30.4 us
    pallas_call x2, Pallas kernels, apply_blocks(): pl.pallas_call(functools.partial(apply_kernel, first), out_shape=(jax.Sha...  24.7 us
    pallas_call x1, Pallas kernels, next_terms(): pl.pallas_call(next_terms_kernel, out_shape=jax.ShapeDtypeStruct((x.shape...  9.95 us

profile of v2, /device:TPU:0, one launch (start us, length us, event | category | flops | bytes accessed | tf_op | source)
XLA Modules:
  0.0 438.9 jit_solution(18353145389095843627)
XLA Ops:
  0.6 0.7 multiply_add_fusion.1
  1.3 0.1 pad.7.clone
  1.4 0.1 pad.12.clone
  1.5 0.7 pad_add_fusion
  2.1 0.6 pad.4.x_ref
  2.7 0.7 broadcast_in_dim.12.w_ref
  3.4 14.4 %shard_map.68 = s32[4,8,8,128]{3,2,1,0:T(8,128)} custom-call(s32[8,128]{1,0:T(8,128)} %pad.4.x_ref), custom_call_target="tpu_custom_call" | custom-call | tf_op jit(solution)/shard_map/pallas_call | solution.py:71
  17.9 1.0 fusion
  18.9 0.1 reshape.17
  19.0 0.1 dynamic-slice_subtract_fusion
  19.1 0.6 reshape.18.index_ref
  19.7 0.7 sub.22.cols_ref
  20.4 4.1 shard_map.69.x_ref
  24.5 30.4 %shard_map.70.x_ref = bf16[72,128,128]{2,1,0:T(8,128)(2,1)} custom-call(bf16[72,128,128]{2,1,0:T(8,128)(2,1)} %shard_map.69.x_ref), custom_call_target="tpu_custom_call" | custom-call | tf_op jit(solution)/shard_map/pallas_call | solution.py:127
  55.0 7.9 %shard_map.71.refs_0_ = bf16[72,128,128]{2,1,0:T(8,128)(2,1)} custom-call(s32[72]{0:T(128)} %sub.22.cols_ref, bf16[72,128,128]{2,1,0:T(8,128)(2,1)} %shard_map.70.x_ref, bf16[128,12288]{1,0:T(8,128)(2,1)} %t_ref.3, f32[128,128]{1,0:T(8,128)} %broadcast_in_dim.12.w_ref), custom_call_target="tpu_custom_call" | custom-call | tf_op jit(solution)/shard_map/pallas_call | solution.py:161
  62.9 143.0 %shard_map.72 = (bf16[72,128,128]{2,1,0:T(8,128)(2,1)}, bf16[18,128,128]{2,1,0:T(8,128)(2,1)}, f32[8,128]{1,0:T(8,128)}) custom-call(bf16[72,128,128]{2,1,0:T(8,128)(2,1)} %shard_map.71.refs_0_), custom_call_target="tpu_custom_call" | custom-call | tf_op jit(solution)/shard_map/pallas_call | solution.py:326
  205.9 0.7 slice.45
  206.6 11.1 %shard_map.73 = (f32[128,12288]{1,0:T(8,128)}, f32[8,128]{1,0:T(8,128)}) custom-call(s32[72]{0:T(128)} %sub.22.cols_ref, bf16[72,128,128]{2,1,0:T(8,128)(2,1)} %shard_map.70.x_ref, bf16[72,128,128]{2,1,0:T(8,128)(2,1)} %get-tuple-element.13.d_ref.refs_2_, f32[128,128]{1,0:T(8,128)} %broadcast_in_dim.12.w_ref), custom_call_target="tpu_custom_call" | custom-call | tf_op jit(solution)/shard_map/pallas_call | solution.py:386
  217.6 0.7 slice.46
  218.3 0.7 maximum_maximum_fusion.x_ref
  218.9 13.5 %shard_map.74 = f32[4,8,8,128]{3,2,1,0:T(8,128)} custom-call(f32[8,128]{1,0:T(8,128)} %maximum_maximum_fusion.x_ref), custom_call_target="tpu_custom_call" | custom-call | tf_op jit(solution)/shard_map/pallas_call | solution.py:71
  232.5 1.1 reduce_sum.18
  233.6 0.6 fusion.2
  236.0 0.6 pad_maximum_fusion.scale_ref.refs_0_
  236.7 9.9 %shard_map.75.refs_1_ = bf16[72,128,128]{2,1,0:T(8,128)(2,1)} custom-call(s32[72]{0:T(128)} %sub.22.cols_ref, f32[2]{0:T(128)} %pad_maximum_fusion.scale_ref.refs_0_, bf16[72,128,128]{2,1,0:T(8,128)(2,1)} %shard_map.70.x_ref, bf16[128,12288]{1,0:T(8,128)(2,1)} %t_ref.3, f32[128,12288]{1,0:T(8,128)} %get-tuple-element.15.image_ref.refs_0_, ...), custom_call_target="tpu_custom_call" | custom-call | tf_op jit(solution)/shard_map/pallas_call | solution.py:186
  246.6 148.8 %shard_map.76 = (bf16[72,128,128]{2,1,0:T(8,128)(2,1)}, bf16[18,128,128]{2,1,0:T(8,128)(2,1)}, f32[8,128]{1,0:T(8,128)}) custom-call(f32[2]{0:T(128)} %pad_maximum_fusion.scale_ref.refs_0_, bf16[72,128,128]{2,1,0:T(8,128)(2,1)} %shard_map.75.refs_1_, bf16[72,128,128]{2,1,0:T(8,128)(2,1)} %get-tuple-element.13.d_ref.refs_2_), custom_call_target="tpu_custom_call" | custom-call | tf_op jit(solution)/shard_map/pallas_call | solution.py:326
  395.4 0.7 slice.50
  396.1 0.0 copy-start
  396.1 13.7 %shard_map.77 = (f32[128,12288]{1,0:T(8,128)}, f32[8,128]{1,0:T(8,128)}) custom-call(s32[72]{0:T(128)} %sub.22.cols_ref, bf16[72,128,128]{2,1,0:T(8,128)(2,1)} %shard_map.70.x_ref, bf16[72,128,128]{2,1,0:T(8,128)(2,1)} %get-tuple-element.17.d_ref, f32[128,128]{1,0:T(8,128)} %broadcast_in_dim.12.w_ref, f32[128,12288]{1,0:T(8,128)} %get-tuple-element.15.image_ref.refs_0_), custom_call_target="tpu_custom_call" | custom-call | tf_op jit(solution)/shard_map/pallas_call | solution.py:386
  409.8 0.7 slice.51
  410.4 0.7 maximum_maximum_fusion.1.x_ref
  411.1 10.5 %shard_map.78 = f32[4,8,8,128]{3,2,1,0:T(8,128)} custom-call(f32[8,128]{1,0:T(8,128)} %maximum_maximum_fusion.1.x_ref), custom_call_target="tpu_custom_call" | custom-call | tf_op jit(solution)/shard_map/pallas_call | solution.py:71
  421.6 1.1 reduce_sum.19
  422.6 0.7 fusion.1
  429.0 0.0 copy-done
  429.0 0.0 copy-start.1
  429.1 0.0 copy-start.2
  429.1 8.6 %multiply_subtract_fusion = f32[128,12288]{1,0:T(8,128)} fusion(f32[128,12288]{1,0:T(8,128)} %get-tuple-element.21, f32[128,12288]{1,0:T(8,128)} %get-tuple-element.15.image_ref.refs_0_, bf16[128,12288]{1,0:T(8,128)(2,1)S(1)} %copy-done, f32[]{:T(128)S(6)} %div.19, f32[]{:T(128)S(6)} %add.49), kind=kLoop, calls=%fused_computation | loop fusion | flops 7864320 | bytes 22020104 | tf_op jit(solution)/shard_map/sub | solution.py:444
  437.7 0.0 copy-done.1
  437.7 0.0 copy-done.2
  437.7 1.2 multiply_add_fusion
  (4 shorter events, 0.0 us)
Async XLA Ops:
  396.1 33.0 %copy-start = (bf16[128,12288]{1,0:T(8,128)(2,1)S(1)}, bf16[128,12288]{1,0:T(8,128)(2,1)}, u32[]{:S(2)}) copy-start(bf16[128,12288]{1,0:T(8,128)(2,1)} %t_ref.3) | copy-start | bytes 9437188
  429.0 8.6 %copy-start.1 = (bf16[18,128,128]{2,1,0:T(8,128)(2,1)S(1)}, bf16[18,128,128]{2,1,0:T(8,128)(2,1)}, u32[]{:S(2)}) copy-start(bf16[18,128,128]{2,1,0:T(8,128)(2,1)} %get-tuple-element.19) | copy-start | bytes 1769476
  429.1 8.6 %copy-start.2 = (bf16[18,128,128]{2,1,0:T(8,128)(2,1)S(1)}, bf16[18,128,128]{2,1,0:T(8,128)(2,1)}, u32[]{:S(2)}) copy-start(bf16[18,128,128]{2,1,0:T(8,128)(2,1)} %get-tuple-element.20) | copy-start | bytes 1769476

commit v3 on v2

--- a/solution.py
+++ b/solution.py
@@ -12,6 +12,7 @@
 T_STEPS = 64
 RIDGE_SHARE = 0.2
 LANES = 128
+LAG = 2
 VMEM = pltpu.VMEM
 F32 = jnp.float32
 BF16 = jnp.bfloat16
@@ -263,7 +264,7 @@
             total = total - shift * before_ref[b].astype(F32)
         return total
 
-    def piece(p, carry):
+    def pass_right(p):
         @pl.when(has_left)
         def _():
             rightward(to_right, p).wait_recv()
@@ -273,6 +274,7 @@
                 add(from_left, to_right, p)
                 rightward(to_right, p).start()
 
+    def pass_left(p):
         @pl.when(has_right)
         def _():
             leftward(to_left, p).wait_recv()
@@ -282,15 +284,30 @@
                 add(from_right, to_left, p)
                 leftward(to_left, p).start()
 
-        def one(i, inner):
-            b = p * size + i
-            out_ref[b] = total_of(b).astype(BF16)
-            return inner
-
-        lax.fori_loop(0, size, one, 0)
-        return carry
-
-    lax.fori_loop(0, pieces, piece, 0)
+    low = me * 2 < n
+
+    def piece(q, carry):
+        @pl.when(q < pieces)
+        def _():
+            pl.when(low)(lambda: pass_right(q))
+            pl.when(jnp.logical_not(low))(lambda: pass_left(q))
+
+        @pl.when(q >= LAG)
+        def _():
+            p = q - LAG
+            pl.when(low)(lambda: pass_left(p))
+            pl.when(jnp.logical_not(low))(lambda: pass_right(p))
+
+            def one(i, inner):
+                b = p * size + i
+                out_ref[b] = total_of(b).astype(BF16)
+                return inner
+
+            lax.fori_loop(0, size, one, 0)
+
+        return carry
+
+    lax.fori_loop(0, pieces + LAG, piece, 0)
     sums_ref[...] = jnp.zeros_like(sums_ref)
 
     def own(i, carry):
@@ -319,7 +336,7 @@
 def sweep(terms, scale, before, call_id):
     n = lax.axis_size("row")
     share = terms.shape[0] // n
-    pieces = math.gcd(terms.shape[0], 12)
+    pieces = math.gcd(terms.shape[0], 24)
     first = before is None
     sems = pltpu.SemaphoreType.DMA((pieces,))
     whole = VMEM(terms.shape, BF16)

time: 439 us -> 280 us (0.64)
  Pallas kernels: 407 us -> 248 us
    pallas_call x2, Pallas kernels: 292 us -> 135 us  [sweep(): pl.pallas_call(functools.partial(sweep_kernel, first), out_shape=(jax.Sha...]
where the time goes in v3:
time: 280 us; the launch traced here: 279 us
  Pallas kernels  248 us (89%)
  other arithmetic  15.3 us (5%)
  between operations  8.3 us (3%)
  local copies, waits for them, and re-layouts  7.86 us (3%)
    pallas_call x2, Pallas kernels, sweep(): pl.pallas_call(functools.partial(sweep_kernel, first), out_shape=(jax.Sha...  135 us
    pallas_call x3, Pallas kernels, gather_small(): pl.pallas_call(gather_small_kernel, out_shape=jax.ShapeDtypeStruct((rows,...  36.2 us
    pallas_call x1, Pallas kernels, exchange_blocks(): pl.pallas_call(functools.partial(exchange_kernel, x.shape[0] // n), out_s...  30.4 us
    pallas_call x2, Pallas kernels, apply_blocks(): pl.pallas_call(functools.partial(apply_kernel, first), out_shape=(jax.Sha...  24.7 us
    pallas_call x1, Pallas kernels, next_terms(): pl.pallas_call(next_terms_kernel, out_shape=jax.ShapeDtypeStruct((x.shape...  9.95 us
    sub x1, other arithmetic, on_device(): residual = targets.astype(F32) - mixed * image0 - alpha1 * image1  8.61 us
    pallas_call x1, Pallas kernels, first_terms(): pl.pallas_call(first_terms_kernel, out_shape=jax.ShapeDtypeStruct((x.shap...  7.93 us

profile of v3, /device:TPU:0, one launch (start us, length us, event | category | flops | bytes accessed | tf_op | source)
XLA Modules:
  0.0 279.4 jit_solution(5308835808640161850)
XLA Ops:
  0.6 0.7 multiply_add_fusion.1
  1.3 0.1 pad.7.clone
  1.4 0.1 pad.12.clone
  1.5 0.7 pad_add_fusion
  2.1 0.6 pad.4.x_ref
  2.7 0.7 broadcast_in_dim.12.w_ref
  3.4 14.4 %shard_map.68 = s32[4,8,8,128]{3,2,1,0:T(8,128)} custom-call(s32[8,128]{1,0:T(8,128)} %pad.4.x_ref), custom_call_target="tpu_custom_call" | custom-call | tf_op jit(solution)/shard_map/pallas_call | solution.py:72
  17.9 1.0 fusion
  18.9 0.1 reshape.17
  19.0 0.1 dynamic-slice_subtract_fusion
  19.1 0.6 reshape.18.index_ref
  19.7 0.7 sub.22.cols_ref
  20.4 4.1 %shard_map.69.x_ref = bf16[72,128,128]{2,1,0:T(8,128)(2,1)} custom-call(s32[72]{0:T(128)} %reshape.18.index_ref, bf16[128,12288]{1,0:T(8,128)(2,1)} %x_ref.1), custom_call_target="tpu_custom_call" | custom-call | tf_op jit(solution)/shard_map/pallas_call | solution.py:96
  24.5 30.4 %shard_map.70.x_ref = bf16[72,128,128]{2,1,0:T(8,128)(2,1)} custom-call(bf16[72,128,128]{2,1,0:T(8,128)(2,1)} %shard_map.69.x_ref), custom_call_target="tpu_custom_call" | custom-call | tf_op jit(solution)/shard_map/pallas_call | solution.py:128
  55.0 7.9 %shard_map.71.refs_0_ = bf16[72,128,128]{2,1,0:T(8,128)(2,1)} custom-call(s32[72]{0:T(128)} %sub.22.cols_ref, bf16[72,128,128]{2,1,0:T(8,128)(2,1)} %shard_map.70.x_ref, bf16[128,12288]{1,0:T(8,128)(2,1)} %t_ref.3, f32[128,128]{1,0:T(8,128)} %broadcast_in_dim.12.w_ref), custom_call_target="tpu_custom_call" | custom-call | tf_op jit(solution)/shard_map/pallas_call | solution.py:162
  62.9 67.6 %shard_map.72 = (bf16[72,128,128]{2,1,0:T(8,128)(2,1)}, bf16[18,128,128]{2,1,0:T(8,128)(2,1)}, f32[8,128]{1,0:T(8,128)}) custom-call(bf16[72,128,128]{2,1,0:T(8,128)(2,1)} %shard_map.71.refs_0_), custom_call_target="tpu_custom_call" | custom-call | tf_op jit(solution)/shard_map/pallas_call | solution.py:343
  130.5 0.7 slice.45
  131.1 11.0 %shard_map.73 = (f32[128,12288]{1,0:T(8,128)}, f32[8,128]{1,0:T(8,128)}) custom-call(s32[72]{0:T(128)} %sub.22.cols_ref, bf16[72,128,128]{2,1,0:T(8,128)(2,1)} %shard_map.70.x_ref, bf16[72,128,128]{2,1,0:T(8,128)(2,1)} %get-tuple-element.13.d_ref.refs_2_, f32[128,128]{1,0:T(8,128)} %broadcast_in_dim.12.w_ref), custom_call_target="tpu_custom_call" | custom-call | tf_op jit(solution)/shard_map/pallas_call | solution.py:403
  142.2 0.7 slice.46
  142.9 0.7 maximum_maximum_fusion.x_ref
  143.5 11.4 %shard_map.74 = f32[4,8,8,128]{3,2,1,0:T(8,128)} custom-call(f32[8,128]{1,0:T(8,128)} %maximum_maximum_fusion.x_ref), custom_call_target="tpu_custom_call" | custom-call | tf_op jit(solution)/shard_map/pallas_call | solution.py:72
  154.9 1.1 reduce_sum.18
  155.9 0.6 fusion.2
  158.4 0.6 pad_maximum_fusion.scale_ref.refs_0_
  159.1 9.9 %shard_map.75.refs_1_ = bf16[72,128,128]{2,1,0:T(8,128)(2,1)} custom-call(s32[72]{0:T(128)} %sub.22.cols_ref, f32[2]{0:T(128)} %pad_maximum_fusion.scale_ref.refs_0_, bf16[72,128,128]{2,1,0:T(8,128)(2,1)} %shard_map.70.x_ref, bf16[128,12288]{1,0:T(8,128)(2,1)} %t_ref.3, f32[128,12288]{1,0:T(8,128)} %get-tuple-element.15.image_ref.refs_0_, ...), custom_call_target="tpu_custom_call" | custom-call | tf_op jit(solution)/shard_map/pallas_call | solution.py:187
  169.0 67.0 %shard_map.76 = (bf16[72,128,128]{2,1,0:T(8,128)(2,1)}, bf16[18,128,128]{2,1,0:T(8,128)(2,1)}, f32[8,128]{1,0:T(8,128)}) custom-call(f32[2]{0:T(128)} %pad_maximum_fusion.scale_ref.refs_0_, bf16[72,128,128]{2,1,0:T(8,128)(2,1)} %shard_map.75.refs_1_, bf16[72,128,128]{2,1,0:T(8,128)(2,1)} %get-tuple-element.13.d_ref.refs_2_), custom_call_target="tpu_custom_call" | custom-call | tf_op jit(solution)/shard_map/pallas_call | solution.py:343
  236.0 0.7 slice.50
  236.7 0.0 copy-start
  236.7 13.7 %shard_map.77 = (f32[128,12288]{1,0:T(8,128)}, f32[8,128]{1,0:T(8,128)}) custom-call(s32[72]{0:T(128)} %sub.22.cols_ref, bf16[72,128,128]{2,1,0:T(8,128)(2,1)} %shard_map.70.x_ref, bf16[72,128,128]{2,1,0:T(8,128)(2,1)} %get-tuple-element.17.d_ref, f32[128,128]{1,0:T(8,128)} %broadcast_in_dim.12.w_ref, f32[128,12288]{1,0:T(8,128)} %get-tuple-element.15.image_ref.refs_0_), custom_call_target="tpu_custom_call" | custom-call | tf_op jit(solution)/shard_map/pallas_call | solution.py:403
  250.3 0.7 slice.51
  251.0 0.7 maximum_maximum_fusion.1.x_ref
  251.7 10.5 %shard_map.78 = f32[4,8,8,128]{3,2,1,0:T(8,128)} custom-call(f32[8,128]{1,0:T(8,128)} %maximum_maximum_fusion.1.x_ref), custom_call_target="tpu_custom_call" | custom-call | tf_op jit(solution)/shard_map/pallas_call | solution.py:72
  262.1 1.1 reduce_sum.19
  263.2 0.7 fusion.1
  269.6 0.0 copy-done
  269.6 0.0 copy-start.1
  269.6 0.0 copy-start.2
  269.6 8.6 %multiply_subtract_fusion = f32[128,12288]{1,0:T(8,128)} fusion(f32[128,12288]{1,0:T(8,128)} %get-tuple-element.21, f32[128,12288]{1,0:T(8,128)} %get-tuple-element.15.image_ref.refs_0_, bf16[128,12288]{1,0:T(8,128)(2,1)S(1)} %copy-done, f32[]{:T(128)S(6)} %div.19, f32[]{:T(128)S(6)} %add.49), kind=kLoop, calls=%fused_computation | loop fusion | flops 7864320 | bytes 22020104 | tf_op jit(solution)/shard_map/sub | solution.py:461
  278.2 0.0 copy-done.1
  278.2 0.0 copy-done.2
  278.2 1.2 multiply_add_fusion
  (4 shorter events, 0.0 us)
Async XLA Ops:
  236.7 32.9 %copy-start = (bf16[128,12288]{1,0:T(8,128)(2,1)S(1)}, bf16[128,12288]{1,0:T(8,128)(2,1)}, u32[]{:S(2)}) copy-start(bf16[128,12288]{1,0:T(8,128)(2,1)} %t_ref.3) | copy-start | bytes 9437188
  269.6 8.6 %copy-start.1 = (bf16[18,128,128]{2,1,0:T(8,128)(2,1)S(1)}, bf16[18,128,128]{2,1,0:T(8,128)(2,1)}, u32[]{:S(2)}) copy-start(bf16[18,128,128]{2,1,0:T(8,128)(2,1)} %get-tuple-element.19) | copy-start | bytes 1769476
  269.6 8.6 %copy-start.2 = (bf16[18,128,128]{2,1,0:T(8,128)(2,1)S(1)}, bf16[18,128,128]{2,1,0:T(8,128)(2,1)}, u32[]{:S(2)}) copy-start(bf16[18,128,128]{2,1,0:T(8,128)(2,1)} %get-tuple-element.20) | copy-start | bytes 1769476

commit v4 on v3

--- a/solution.py
+++ b/solution.py
@@ -140,7 +140,7 @@
 
 
 def unroll_of(count):
-    return math.gcd(count, 4)
+    return math.gcd(count, 8)
 
 
 def first_terms_kernel(cols_ref, x_ref, t_ref, w_ref, out_ref):
@@ -370,7 +370,7 @@
         image_ref[:, place] = jnp.zeros((samples, BLOCK), F32)
         return carry
 
-    lax.fori_loop(0, columns, clear, 0, unroll=2)
+    lax.fori_loop(0, columns, clear, 0, unroll=4)
 
     def some(i, carry):
         made = [
@@ -383,18 +383,25 @@
         return carry
 
     lax.fori_loop(0, count // step, some, 0)
-    sums_ref[...] = jnp.zeros_like(sums_ref)
+
+    def fold(values):
+        return jnp.sum(values.reshape(samples // 8, 8, BLOCK), axis=0)
 
     def measure(i, carry):
         place = pl.ds(pl.multiple_of(i * BLOCK, BLOCK), BLOCK)
         image = image_ref[:, place]
         weighted = w_ref[...] * image
-        sums_ref[0:1, :] += jnp.sum(weighted * image, axis=0, keepdims=True)
+        square, cross = carry
+        square = square + fold(weighted * image)
         if before_ref is not None:
-            sums_ref[1:2, :] += jnp.sum(weighted * before_ref[:, place], axis=0, keepdims=True)
-        return carry
-
-    lax.fori_loop(0, columns, measure, 0, unroll=2)
+            cross = cross + fold(weighted * before_ref[:, place])
+        return square, cross
+
+    empty = jnp.zeros((8, BLOCK), F32)
+    square, cross = lax.fori_loop(0, columns, measure, (empty, empty), unroll=4)
+    sums_ref[...] = jnp.zeros_like(sums_ref)
+    sums_ref[0:1, :] = jnp.sum(square, axis=0, keepdims=True)
+    sums_ref[1:2, :] = jnp.sum(cross, axis=0, keepdims=True)
 
 
 def apply_blocks(cols, x, direction, weight, before, taxa):

time: 280 us -> 273 us (0.975)
  Pallas kernels: 248 us -> 241 us
    pallas_call x2, Pallas kernels: 24.7 us -> 20.9 us  [apply_blocks(): pl.pallas_call(functools.partial(apply_kernel, first), out_shape=(jax.Sha...]
where the time goes in v4:
time: 273 us
  Pallas kernels  241 us (88%)
  other arithmetic  15.3 us (6%)
  between operations  8.3 us (3%)
  local copies, waits for them, and re-layouts  7.86 us (3%)
    pallas_call x2, Pallas kernels, sweep(): pl.pallas_call(functools.partial(sweep_kernel, first), out_shape=(jax.Sha...  135 us
    pallas_call x3, Pallas kernels, gather_small(): pl.pallas_call(gather_small_kernel, out_shape=jax.ShapeDtypeStruct((rows,...  36.2 us
    pallas_call x1, Pallas kernels, exchange_blocks(): pl.pallas_call(functools.partial(exchange_kernel, x.shape[0] // n), out_s...  30.4 us
    pallas_call x2, Pallas kernels, apply_blocks(): pl.pallas_call(functools.partial(apply_kernel, first), out_shape=(jax.Sha...  20.9 us
    sub x1, other arithmetic, on_device(): residual = targets.astype(F32) - mixed * image0 - alpha1 * image1  8.61 us
    pallas_call x1, Pallas kernels, next_terms(): pl.pallas_call(next_terms_kernel, out_shape=jax.ShapeDtypeStruct((x.shape...  8.52 us
    pallas_call x1, Pallas kernels, first_terms(): pl.pallas_call(first_terms_kernel, out_shape=jax.ShapeDtypeStruct((x.shap...  6.45 us

profile of v4, /device:TPU:0, one launch (start us, length us, event | category | flops | bytes accessed | tf_op | source)
XLA Modules:
  0.0 272.7 jit_solution(13258393541523457038)
XLA Ops:
  0.6 0.7 multiply_add_fusion.1
  1.3 0.1 pad.7.clone
  1.4 0.1 pad.12.clone
  1.5 0.7 pad_add_fusion
  2.1 0.6 pad.4.x_ref
  2.7 0.7 broadcast_in_dim.12.w_ref
  3.4 14.4 %shard_map.68 = s32[4,8,8,128]{3,2,1,0:T(8,128)} custom-call(s32[8,128]{1,0:T(8,128)} %pad.4.x_ref), custom_call_target="tpu_custom_call" | custom-call | tf_op jit(solution)/shard_map/pallas_call | solution.py:72
  17.9 1.0 fusion
  18.9 0.1 reshape.17
  19.0 0.1 dynamic-slice_subtract_fusion
  19.1 0.6 reshape.18.index_ref
  19.7 0.7 sub.22.cols_ref
  20.4 4.1 %shard_map.69.x_ref = bf16[72,128,128]{2,1,0:T(8,128)(2,1)} custom-call(s32[72]{0:T(128)} %reshape.18.index_ref, bf16[128,12288]{1,0:T(8,128)(2,1)} %x_ref.1), custom_call_target="tpu_custom_call" | custom-call | tf_op jit(solution)/shard_map/pallas_call | solution.py:96
  24.5 30.4 %shard_map.70.x_ref = bf16[72,128,128]{2,1,0:T(8,128)(2,1)} custom-call(bf16[72,128,128]{2,1,0:T(8,128)(2,1)} %shard_map.69.x_ref), custom_call_target="tpu_custom_call" | custom-call | tf_op jit(solution)/shard_map/pallas_call | solution.py:128
  55.0 6.4 %shard_map.71.refs_0_ = bf16[72,128,128]{2,1,0:T(8,128)(2,1)} custom-call(s32[72]{0:T(128)} %sub.22.cols_ref, bf16[72,128,128]{2,1,0:T(8,128)(2,1)} %shard_map.70.x_ref, bf16[128,12288]{1,0:T(8,128)(2,1)} %t_ref.3, f32[128,128]{1,0:T(8,128)} %broadcast_in_dim.12.w_ref), custom_call_target="tpu_custom_call" | custom-call | tf_op jit(solution)/shard_map/pallas_call | solution.py:162
  61.4 67.6 %shard_map.72 = (bf16[72,128,128]{2,1,0:T(8,128)(2,1)}, bf16[18,128,128]{2,1,0:T(8,128)(2,1)}, f32[8,128]{1,0:T(8,128)}) custom-call(bf16[72,128,128]{2,1,0:T(8,128)(2,1)} %shard_map.71.refs_0_), custom_call_target="tpu_custom_call" | custom-call | tf_op jit(solution)/shard_map/pallas_call | solution.py:343
  129.0 0.7 slice.45
  129.7 9.1 %shard_map.73 = (f32[128,12288]{1,0:T(8,128)}, f32[8,128]{1,0:T(8,128)}) custom-call(s32[72]{0:T(128)} %sub.22.cols_ref, bf16[72,128,128]{2,1,0:T(8,128)(2,1)} %shard_map.70.x_ref, bf16[72,128,128]{2,1,0:T(8,128)(2,1)} %get-tuple-element.13.d_ref.refs_2_, f32[128,128]{1,0:T(8,128)} %broadcast_in_dim.12.w_ref), custom_call_target="tpu_custom_call" | custom-call | tf_op jit(solution)/shard_map/pallas_call | solution.py:410
  138.7 0.7 slice.46
  139.4 0.7 maximum_maximum_fusion.x_ref
  140.1 11.4 %shard_map.74 = f32[4,8,8,128]{3,2,1,0:T(8,128)} custom-call(f32[8,128]{1,0:T(8,128)} %maximum_maximum_fusion.x_ref), custom_call_target="tpu_custom_call" | custom-call | tf_op jit(solution)/shard_map/pallas_call | solution.py:72
  151.4 1.1 reduce_sum.18
  152.5 0.6 fusion.2
  155.0 0.6 pad_maximum_fusion.scale_ref.refs_0_
  155.6 8.5 %shard_map.75.refs_1_ = bf16[72,128,128]{2,1,0:T(8,128)(2,1)} custom-call(s32[72]{0:T(128)} %sub.22.cols_ref, f32[2]{0:T(128)} %pad_maximum_fusion.scale_ref.refs_0_, bf16[72,128,128]{2,1,0:T(8,128)(2,1)} %shard_map.70.x_ref, bf16[128,12288]{1,0:T(8,128)(2,1)} %t_ref.3, f32[128,12288]{1,0:T(8,128)} %get-tuple-element.15.image_ref.refs_0_, ...), custom_call_target="tpu_custom_call" | custom-call | tf_op jit(solution)/shard_map/pallas_call | solution.py:187
  164.1 67.0 %shard_map.76 = (bf16[72,128,128]{2,1,0:T(8,128)(2,1)}, bf16[18,128,128]{2,1,0:T(8,128)(2,1)}, f32[8,128]{1,0:T(8,128)}) custom-call(f32[2]{0:T(128)} %pad_maximum_fusion.scale_ref.refs_0_, bf16[72,128,128]{2,1,0:T(8,128)(2,1)} %shard_map.75.refs_1_, bf16[72,128,128]{2,1,0:T(8,128)(2,1)} %get-tuple-element.13.d_ref.refs_2_), custom_call_target="tpu_custom_call" | custom-call | tf_op jit(solution)/shard_map/pallas_call | solution.py:343
  231.1 0.7 slice.50
  231.8 0.0 copy-start
  231.8 11.8 %shard_map.77 = (f32[128,12288]{1,0:T(8,128)}, f32[8,128]{1,0:T(8,128)}) custom-call(s32[72]{0:T(128)} %sub.22.cols_ref, bf16[72,128,128]{2,1,0:T(8,128)(2,1)} %shard_map.70.x_ref, bf16[72,128,128]{2,1,0:T(8,128)(2,1)} %get-tuple-element.17.d_ref, f32[128,128]{1,0:T(8,128)} %broadcast_in_dim.12.w_ref, f32[128,12288]{1,0:T(8,128)} %get-tuple-element.15.image_ref.refs_0_), custom_call_target="tpu_custom_call" | custom-call | tf_op jit(solution)/shard_map/pallas_call | solution.py:410
  243.6 0.7 slice.51
  244.3 0.7 maximum_maximum_fusion.1.x_ref
  244.9 10.4 %shard_map.78 = f32[4,8,8,128]{3,2,1,0:T(8,128)} custom-call(f32[8,128]{1,0:T(8,128)} %maximum_maximum_fusion.1.x_ref), custom_call_target="tpu_custom_call" | custom-call | tf_op jit(solution)/shard_map/pallas_call | solution.py:72
  255.4 1.1 reduce_sum.19
  256.4 0.7 fusion.1
  262.8 0.0 copy-done
  262.9 0.0 copy-start.1
  262.9 0.0 copy-start.2
  262.9 8.6 %multiply_subtract_fusion = f32[128,12288]{1,0:T(8,128)} fusion(f32[128,12288]{1,0:T(8,128)} %get-tuple-element.21, f32[128,12288]{1,0:T(8,128)} %get-tuple-element.15.image_ref.refs_0_, bf16[128,12288]{1,0:T(8,128)(2,1)S(1)} %copy-done, f32[]{:T(128)S(6)} %div.19, f32[]{:T(128)S(6)} %add.49), kind=kLoop, calls=%fused_computation | loop fusion | flops 7864320 | bytes 22020104 | tf_op jit(solution)/shard_map/sub | solution.py:468
  271.5 0.0 copy-done.1
  271.5 0.0 copy-done.2
  271.5 1.2 multiply_add_fusion
  (4 shorter events, 0.0 us)
Async XLA Ops:
  231.8 31.0 %copy-start = (bf16[128,12288]{1,0:T(8,128)(2,1)S(1)}, bf16[128,12288]{1,0:T(8,128)(2,1)}, u32[]{:S(2)}) copy-start(bf16[128,12288]{1,0:T(8,128)(2,1)} %t_ref.3) | copy-start | bytes 9437188
  262.9 8.6 %copy-start.1 = (bf16[18,128,128]{2,1,0:T(8,128)(2,1)S(1)}, bf16[18,128,128]{2,1,0:T(8,128)(2,1)}, u32[]{:S(2)}) copy-start(bf16[18,128,128]{2,1,0:T(8,128)(2,1)} %get-tuple-element.19) | copy-start | bytes 1769476
  262.9 8.6 %copy-start.2 = (bf16[18,128,128]{2,1,0:T(8,128)(2,1)S(1)}, bf16[18,128,128]{2,1,0:T(8,128)(2,1)}, u32[]{:S(2)}) copy-start(bf16[18,128,128]{2,1,0:T(8,128)(2,1)} %get-tuple-element.20) | copy-start | bytes 1769476
